TPU v7x, 256 devices: a whole 4x4x8 slice. The times are simulated.
256 devices in a mesh: req: 32 (over x, y, z_lo), tp: 8 (over z_hi, core).
Axes of the slice: x: 4, y: 4, z: 8 (z_hi: 4, z_lo: 2; z = z_hi * 2 + z_lo), core: 2. Of those that a mesh axis runs over, the one named last changes fastest.
Arguments:
- hidden_in: bfloat16 [1024, 24, 3072], P(('req', 'tp')), may hold values from -6 to 6
- norm_gain: float32 [3072], replicated, may hold values from 0.1 to 1.9
- w_q: bfloat16 [3072, 3072], P(None, 'tp'), may hold values from -0.108253175 to 0.108253175
- w_k: bfloat16 [3072, 3072], P(None, 'tp'), may hold values from -3.35584844 to 3.35584844
- w_v: bfloat16 [3072, 3072], P(None, 'tp'), may hold values from -0.109375 to 0.109375
- w_o: bfloat16 [3072, 3072], P('tp'), may hold values from -0.109375 to 0.109375
- lengths: int32 [32, 32], P('req'), may hold values from 1 to 24, 576 in all within a row
- dest: int32 [32, 32, 1], P('req'), may hold values from 0 to 31; in each aligned block of 32 rows (0 to 31, 32 to 63, ..., all dimensions but the last counted through in order) at most 2 rows name the same one
Outputs:
- hidden_out: bfloat16 [1024, 24, 3072], P(('req', 'tp'))
- cache: bfloat16 [2048, 24, 2, 3072], P('req', None, None, 'tp')
Inputs may be any that keep to these rules, and one draw needn't show every extreme that they name: Each replica's lengths sum to 576 and the longest is 24. `dest`: no replica names one destination for more than 2 of its requests, and some replica names one exactly 2 times.
All inputs are finite; a program needn't handle non-finite values.
Results may differ from a plain program's by a relative error of at most 0.015.
Values may be sent and summed in bfloat16 or wider, within the bound.
No kernel may reach another device: no remote copies, remote signals or barrier semaphores. Data moves between devices by JAX's collectives and lax.ppermute only.
A program may use at most 128 MiB of HBM per device.

v0:
```python
import jax
import jax.numpy as jnp
from jax import lax
from jax.sharding import PartitionSpec as P

HD = 96
CAP = 2
EPS = 1e-05


def rope_tables(slot):
    pos = jnp.arange(slot, dtype=jnp.float32)
    inv = 10000.0 ** (-(jnp.arange(HD // 2, dtype=jnp.float32) * 2.0) / HD)
    angle = pos[:, None] * inv[None, :]
    cosine = jnp.concatenate([jnp.cos(angle), jnp.cos(angle)], -1)
    sine = jnp.concatenate([jnp.sin(angle), jnp.sin(angle)], -1)
    return (cosine, sine)


def rotate(x, cosine, sine):
    half = HD // 2
    turned = jnp.concatenate([-x[..., half:], x[..., :half]], -1)
    return x * cosine[None, :, None, :] + turned * sine[None, :, None, :]


def on_device(hidden_in, norm_gain, w_q, w_k, w_v, w_o, lengths, dest):
    req_dev, slot, width = hidden_in.shape
    req_rep = req_dev * lax.axis_size("tp")
    per_dev = w_q.shape[1]
    heads_dev = per_dev // HD
    cosine, sine = rope_tables(slot)
    xf = hidden_in.astype(jnp.float32)
    mean_sq = jnp.mean(xf * xf, -1, keepdims=True)
    normed = (xf * lax.rsqrt(mean_sq + EPS) * norm_gain).astype(jnp.bfloat16)
    piece = lax.all_gather(normed, "tp", axis=0, tiled=True)
    count = piece.shape[0]
    flat = piece.reshape(count * slot, width)
    shape4 = (count, slot, heads_dev, HD)
    query = rotate(
        jnp.dot(flat, w_q, preferred_element_type=jnp.float32).reshape(shape4), cosine, sine
    )
    keys = rotate(
        jnp.dot(flat, w_k, preferred_element_type=jnp.float32).reshape(shape4), cosine, sine
    )
    values = jnp.dot(flat, w_v, preferred_element_type=jnp.float32)
    query = query.astype(jnp.bfloat16).reshape(count, slot, per_dev)
    keys = keys.astype(jnp.bfloat16).reshape(count, slot, per_dev)
    values = values.astype(jnp.bfloat16).reshape(count, slot, per_dev)
    projected = jnp.stack([query, keys, values], 2)
    shape4 = (req_rep, slot, heads_dev, HD)
    query = projected[:, :, 0].reshape(shape4)
    keys = projected[:, :, 1]
    values = projected[:, :, 2]
    lens = lengths[0]
    live = jnp.arange(slot, dtype=jnp.int32)[None, :] < lens[:, None]
    causal = jnp.arange(slot)[None, :] <= jnp.arange(slot)[:, None]
    mask = causal[None, None, :, :] & live[:, None, None, :]
    scores = jnp.einsum(
        "rqhd,rkhd->rhqk", query, keys.reshape(shape4), preferred_element_type=jnp.float32
    ) / jnp.sqrt(jnp.float32(HD))
    scores = jnp.where(mask, scores, jnp.float32(-1e30))
    top = jnp.max(scores, -1, keepdims=True)
    expo = jnp.where(mask, jnp.exp(scores - top), 0.0)
    probs = (expo / jnp.sum(expo, -1, keepdims=True)).astype(jnp.bfloat16)
    attn = jnp.einsum(
        "rhqk,rkhd->rqhd", probs, values.reshape(shape4), preferred_element_type=jnp.float32
    )
    attn = attn.astype(jnp.bfloat16).reshape(req_rep, slot, per_dev)
    stacked = jnp.stack([keys, values], 2)
    stacked = jnp.where(live[:, :, None, None], stacked, jnp.zeros_like(stacked))
    target = dest[0, :, 0]
    same = target[:, None] == target[None, :]
    earlier = jnp.arange(req_rep)[None, :] < jnp.arange(req_rep)[:, None]
    rank = jnp.sum((same & earlier).astype(jnp.int32), -1)
    slot_of = target * CAP + rank
    buf_rows = lax.axis_size("req") * CAP
    onehot = (slot_of[None, :] == jnp.arange(buf_rows, dtype=jnp.int32)[:, None]).astype(
        jnp.bfloat16
    )
    outbound = jnp.dot(
        onehot, stacked.reshape(req_rep, slot * 2 * per_dev), preferred_element_type=jnp.float32
    )
    outbound = outbound.astype(jnp.bfloat16).reshape(buf_rows, slot, 2, per_dev)
    cache = lax.all_to_all(outbound, "req", split_axis=0, concat_axis=0, tiled=True)
    part = jnp.dot(
        attn.reshape(req_rep * slot, per_dev), w_o, preferred_element_type=jnp.float32
    ).astype(jnp.bfloat16)
    part = lax.optimization_barrier(part)
    total = lax.psum(
        part.astype(jnp.float32).reshape(req_rep, slot, width).astype(jnp.bfloat16), "tp"
    ).astype(jnp.float32)
    mine = lax.dynamic_slice_in_dim(total, lax.axis_index("tp") * req_dev, req_dev, 0)
    hidden_out = (mine + xf).astype(jnp.bfloat16)
    return (hidden_out, cache)


def solution(mesh):
    placed = (
        P(("req", "tp"), None, None),
        P(),
        P(None, "tp"),
        P(None, "tp"),
        P(None, "tp"),
        P("tp", None),
        P("req", None),
        P("req", None, None),
    )
    return jax.shard_map(
        on_device,
        mesh=mesh,
        in_specs=placed,
        out_specs=(P(("req", "tp"), None, None), P("req", None, None, "tp")),
        check_vma=False,
    )
```

profile of v0, /device:TPU:1, one launch (start us, length us, event | category | flops | bytes accessed | tf_op | source)
XLA Modules:
  0.0 276.4 jit_solution(8190934609367659378)
XLA Ops:
  7.2 0.0 copy-start
  7.2 0.0 all-gather.2.cloned.1.call-start
  7.2 1.4 fusion.11
  8.6 2.1 fusion.13
  10.8 0.0 all-gather.2.cloned.1.call-update
  10.8 0.0 all-reduce.2.cloned.1.call-start
  10.8 4.3 %copy.28 = bf16[3072,384]{0,1:T(8,128)(2,1)} copy(bf16[3072,384]{1,0:T(8,128)(2,1)} %param.10) | data formatting | bytes 4718592 | tf_op args[2]
  15.1 0.0 copy-start.6
  15.1 0.0 copy-start.5
  15.1 4.3 %copy.29 = bf16[3072,384]{0,1:T(8,128)(2,1)} copy(bf16[3072,384]{1,0:T(8,128)(2,1)} %param.11) | data formatting | bytes 4718592 | tf_op args[3]
  19.4 0.1 fusion.23
  19.5 0.1 pad_maximum_fusion
  19.6 0.0 copy-done.6
  19.6 0.2 convert_reduce_fusion
  19.8 0.0 copy-done.5
  19.8 0.1 iota_compare_fusion.3
  19.8 0.2 broadcast_and_fusion
  20.0 52.5 %all-gather.2.cloned.1.call-done = bf16[32,24,3072]{2,1,0:T(8,128)(2,1)} async-done(((bf16[4,24,3072]{2,1,0:T(8,128)(2,1)}), bf16[32,24,3072]{2,1,0:T(8,128)(2,1)}) %all-gather.2.cloned.1.call-update) | async-done | bytes 4718608 | tf_op jit(solution)/shard_map/all_gather | solution.py:35
  72.5 5.7 %convolution_convert_fusion.3 = bf16[768,384]{1,0:T(8,128)(2,1)S(1)} fusion(bf16[768,3072]{1,0:T(8,128)(2,1)} %bitcast.38, bf16[3072,384]{1,0:T(8,128)(2,1)} %param.12), kind=kOutput, calls=%fused_computation.23 | convolution fusion | flops 1812234240 | bytes 7667712 | tf_op jit(solution)/shard_map/dot_general | solution.py:45
  78.2 0.0 copy-start.4
  78.2 1.5 reshape_squeeze_stack_reshape.3
  79.7 5.2 %fusion.1 = f32[32,24,4,96]{3,1,2,0:T(8,128)S(1)} fusion(bf16[4,96,3072,1]{2,1,0,3:T(8,128)(2,1)} %bitcast.35, bf16[32,24,3072]{2,1,0:T(8,128)(2,1)} %all-gather.2.cloned.1.call-done), kind=kOutput, calls=%fused_computation.3 | convolution fusion | flops 1811939328 | bytes 8257536 | tf_op jit(solution)/shard_map/dot_general | solution.py:43
  84.9 0.0 copy-done.4
  84.9 0.6 slice_negate_fusion
  85.5 0.5 fusion.9
  86.0 1.2 copy.33
  87.2 2.5 stack_reshape.6
  89.6 1.5 maximum_select_fusion
  91.1 2.2 copy.34
  93.4 2.8 %select_n.23 = bf16[32,18432]{1,0:T(8,128)(2,1)} reshape(bf16[32,24,2,384]{3,2,1,0:T(2,128)(2,1)} %copy.34) | data formatting | bytes 2359296 | tf_op jit(solution)/shard_map/jit(_where)/select_n | solution.py:70
  96.1 5.4 %fusion.3 = f32[32,24,4,96]{3,1,2,0:T(8,128)S(1)} fusion(bf16[4,96,3072,1]{2,1,0,3:T(8,128)(2,1)} %bitcast.34, bf16[32,24,3072]{2,1,0:T(8,128)(2,1)} %all-gather.2.cloned.1.call-done), kind=kOutput, calls=%fused_computation.5 | convolution fusion | flops 1811939328 | bytes 8257536 | tf_op jit(solution)/shard_map/dot_general | solution.py:40
  101.6 0.0 copy-start.1
  101.6 2.3 slice_negate_fusion.1
  103.8 0.0 copy-done.1
  103.8 4.9 %fusion.25 = (f32[32,4,24]{2,1,0:T(4,128)S(1)}, f32[32,4,24,24]{2,3,1,0:T(8,128)}) fusion(pred[32,24,24]{1,2,0:T(8,128)(4,1)S(1)} %broadcast_and_fusion, bf16[32,24,4,96]{3,1,2,0:T(8,128)(2,1)S(1)} %fusion.9, f32[32,24,4,48]{3,1,2,0:T(8,128)} %get-tuple-element.3, f32[32,24,4,48]{3,1,2,0:T(8,128)} %get-tuple-element.2, f32[32,24,4,96]{3,1,2,0:T(8,128)} %copy-done.1, ...), kind=kOutput, calls=%fused_computation.51 | convolution fusion | flops 15998999 | bytes 3293184 | tf_op jit(solution)/shard_map/sub | solution.py:63
  108.7 2.3 fusion.10
  111.0 0.3 copy.32
  111.3 1.3 reshape_reshape.3
  112.7 0.0 copy-done
  112.7 5.4 %convolution_convert_fusion.1 = bf16[768,3072]{1,0:T(8,128)(2,1)} fusion(bf16[768,384]{1,0:T(8,128)(2,1)} %reshape_reshape.3, bf16[384,3072]{1,0:T(8,128)(2,1)S(1)} %copy-done), kind=kOutput, calls=%fused_computation.2 | convolution fusion | flops 1814298624 | bytes 7667712 | tf_op jit(solution)/shard_map/dot_general | solution.py:85
  118.1 0.0 copy-start.3
  118.1 0.0 all-reduce.2.cloned.1.call-update
  118.1 1.2 copy-done.3
  119.4 2.2 convolution_convert_fusion
  121.5 4.6 %reshape.117 = bf16[64,24,2,384]{3,2,1,0:T(2,128)(2,1)} reshape(bf16[64,18432]{1,0:T(8,128)(2,1)} %convolution_convert_fusion) | data formatting | bytes 4718592 | tf_op jit(solution)/shard_map/reshape | solution.py:83
  126.2 0.0 copy-start.2
  126.2 7.6 %all-to-all-start = ((bf16[64,24,2,384]{3,2,1,0:T(2,128)(2,1)}), bf16[64,24,2,384]{3,2,1,0:T(2,128)(2,1)}, u32[]{:S(2)}, u32[]{:S(2)}) async-start(bf16[64,24,2,384]{3,2,1,0:T(2,128)(2,1)} %reshape.117), calls=%async_computation | async-start | bytes 4718592 | tf_op jit(solution)/shard_map/all_to_all | solution.py:84
  133.7 61.5 %all-to-all-done = bf16[64,24,2,384]{3,2,1,0:T(2,128)(2,1)} async-done(((bf16[64,24,2,384]{3,2,1,0:T(2,128)(2,1)}), bf16[64,24,2,384]{3,2,1,0:T(2,128)(2,1)}, u32[]{:S(2)}, u32[]{:S(2)}) %all-to-all-start) | async-done | bytes 2359328 | tf_op jit(solution)/shard_map/all_to_all | solution.py:84
  195.3 67.5 %all-reduce.2.cloned.1.call-done = bf16[32,24,3072]{2,1,0:T(8,128)(2,1)} async-done(((bf16[32,24,3072]{2,1,0:T(8,128)(2,1)}), bf16[32,24,3072]{2,1,0:T(8,128)(2,1)}) %all-reduce.2.cloned.1.call-update) | async-done | bytes 4718608 | tf_op jit(solution)/shard_map/psum | solution.py:89
  262.8 0.0 copy-done.2
  262.8 2.0 fusion.14
  264.8 4.7 %copy.41 = bf16[64,24,2,384]{3,2,1,0:T(2,128)(2,1)} copy(bf16[64,24,2,384]{3,2,1,0:T(2,128)(2,1)} %all-to-all-done) | data formatting | bytes 4718592
  (4 shorter events, 0.0 us)
Async XLA Ops:
  7.2 105.5 %copy-start = (bf16[384,3072]{1,0:T(8,128)(2,1)S(1)}, bf16[384,3072]{1,0:T(8,128)(2,1)}, u32[]{:S(2)}) copy-start(bf16[384,3072]{1,0:T(8,128)(2,1)} %param.13) | copy-start | bytes 7077892
  7.2 65.3 %all-gather.2.cloned.1.call-start = ((), (), s32[]{:S(2)}) async-start(), calls=%async_computation.1 | async-start | bytes 5308416 | tf_op jit(solution)/shard_map/all_gather | solution.py:35
  10.8 252.0 %all-reduce.2.cloned.1.call-start = ((), (), s32[]{:S(2)}) async-start(), calls=%async_computation.2 | async-start | bytes 9437184 | tf_op jit(solution)/shard_map/psum | solution.py:89
  15.1 4.5 %copy-start.6 = (s32[1,32,1]{1,2,0:T(1,128)S(1)}, s32[1,32,1]{1,2,0:T(1,128)}, u32[]{:S(2)}) copy-start(s32[1,32,1]{1,2,0:T(1,128)} %param.15) | copy-start | bytes 388
  15.1 4.7 %copy-start.5 = (s32[1,32]{1,0:T(1,128)S(1)}, s32[1,32]{1,0:T(1,128)}, u32[]{:S(2)}) copy-start(s32[1,32]{1,0:T(1,128)} %param.14) | copy-start | bytes 388
  78.2 6.7 %copy-start.4 = (bf16[768,384]{1,0:T(8,128)(2,1)}, bf16[768,384]{1,0:T(8,128)(2,1)S(1)}, u32[]{:S(2)}) copy-start(bf16[768,384]{1,0:T(8,128)(2,1)S(1)} %convolution_convert_fusion.3) | copy-start | bytes 1769476
  101.6 2.3 copy-start.1
  118.1 1.3 copy-start.3
  126.2 136.7 %copy-start.2 = (bf16[4,24,3072]{2,1,0:T(8,128)(2,1)S(1)}, bf16[4,24,3072]{2,1,0:T(8,128)(2,1)}, u32[]{:S(2)}) copy-start(bf16[4,24,3072]{2,1,0:T(8,128)(2,1)} %param.8) | copy-start | bytes 1769476
  126.2 69.1 %all-to-all-start = ((bf16[64,24,2,384]{3,2,1,0:T(2,128)(2,1)}), bf16[64,24,2,384]{3,2,1,0:T(2,128)(2,1)}, u32[]{:S(2)}, u32[]{:S(2)}) async-start(bf16[64,24,2,384]{3,2,1,0:T(2,128)(2,1)} %reshape.117), calls=%async_computation | async-start | bytes 4718592 | tf_op jit(solution)/shard_map/all_to_all | solution.py:84
Sparse Core Ops, SparseCore 0:
  10.9 61.5 all-gather.1
  118.2 144.5 all-reduce.1
where the time goes:
time: 277 us; the launch traced here: 276 us
  waiting for transfers between devices  182 us (66%)
  matrix products  31.1 us (11%)
  local copies, waits for them, and re-layouts  30.9 us (11%)
  between operations  14.2 us (5%)
  other arithmetic  11 us (4%)
  starting transfers between devices  7.64 us (3%)
    psum x1, waiting for transfers between devices, on_device(): lax.psum(part.astype(jnp.float32).reshape(req_rep, slot, width).astype(jn...  67.5 us
    all_to_all x1, waiting for transfers between devices, on_device(): lax.all_to_all(outbound, 'req', split_axis=0, concat_axis=0, tiled=True)  61.5 us
    all_gather x1, waiting for transfers between devices, on_device(): piece = lax.all_gather(normed, 'tp', axis=0, tiled=True)  52.5 us
    unnamed x17, local copies, waits for them, and re-layouts  14.5 us
    all_to_all x1, starting transfers between devices, on_device(): lax.all_to_all(outbound, 'req', split_axis=0, concat_axis=0, tiled=True)  7.56 us
    dot_general x1, matrix products, on_device(): values = jnp.dot(flat, w_v, preferred_element_type=jnp.float32)  5.69 us
  transfers between devices with their start and end apart: 3, of which 3 were waited for; matrix products, arithmetic and copies ran while one was open for 6% of the time, Pallas kernels for 0%

commit v1 on v0

--- a/solution.py
+++ b/solution.py
@@ -2,6 +2,7 @@
 import jax.numpy as jnp
 from jax import lax
 from jax.sharding import PartitionSpec as P
+from jax.lax import all_to_all, axis_size
 
 HD = 96
 CAP = 2
@@ -32,7 +33,12 @@
     xf = hidden_in.astype(jnp.float32)
     mean_sq = jnp.mean(xf * xf, -1, keepdims=True)
     normed = (xf * lax.rsqrt(mean_sq + EPS) * norm_gain).astype(jnp.bfloat16)
-    piece = lax.all_gather(normed, "tp", axis=0, tiled=True)
+    piece = jnp.concatenate(
+        all_to_all(
+            jnp.stack([normed] * axis_size("tp")), axis_name="tp", split_axis=0, concat_axis=0
+        ),
+        axis=0,
+    )
     count = piece.shape[0]
     flat = piece.reshape(count * slot, width)
     shape4 = (count, slot, heads_dev, HD)

time: 277 us -> 329 us (1.19)
  waiting for transfers between devices: 182 us -> 211 us
  starting transfers between devices: 7.64 us -> 25.1 us
    all_to_all x0 -> x1, waiting for transfers between devices: none -> 90.7 us  [on_device(): all_to_all(jnp.stack([normed] * axis_size('tp')), axis_name='tp', split_a...]
    all_gather x1 -> x0, waiting for transfers between devices: 52.5 us -> none  [on_device(): piece = lax.all_gather(normed, 'tp', axis=0, tiled=True)]
    all_to_all x0 -> x1, starting transfers between devices: none -> 9.97 us  [on_device(): all_to_all(jnp.stack([normed] * axis_size('tp')), axis_name='tp', split_a...]
    all_to_all x1, starting transfers between devices: 7.56 us -> 15.1 us  [on_device(): lax.all_to_all(outbound, 'req', split_axis=0, concat_axis=0, tiled=True)]
    psum x1, waiting for transfers between devices: 67.5 us -> 62.1 us  [on_device(): lax.psum(part.astype(jnp.float32).reshape(req_rep, slot, width).astype(jn...]
    unnamed x17 -> x23, local copies, waits for them, and re-layouts: 14.5 us -> 16.5 us
  transfers between devices with their start and end apart: 3 -> 3, of which waited for: 3 -> 3; matrix products, arithmetic and copies ran while one was open for 6% -> 7% of each run, Pallas kernels for 0% -> 0%
where the time goes in v1:
time: 329 us; the launch traced here: 328 us
  waiting for transfers between devices  211 us (64%)
  local copies, waits for them, and re-layouts  32.6 us (10%)
  matrix products  30.7 us (9%)
  starting transfers between devices  25.1 us (8%)
  other arithmetic  14.2 us (4%)
  between operations  14.2 us (4%)
    all_to_all x1, waiting for transfers between devices, on_device(): all_to_all(jnp.stack([normed] * axis_size('tp')), axis_name='tp', split_a...  90.7 us
    psum x1, waiting for transfers between devices, on_device(): lax.psum(part.astype(jnp.float32).reshape(req_rep, slot, width).astype(jn...  62.1 us
    all_to_all x1, waiting for transfers between devices, on_device(): lax.all_to_all(outbound, 'req', split_axis=0, concat_axis=0, tiled=True)  58.4 us
    unnamed x23, local copies, waits for them, and re-layouts  16.5 us
    all_to_all x1, starting transfers between devices, on_device(): lax.all_to_all(outbound, 'req', split_axis=0, concat_axis=0, tiled=True)  15.1 us
    all_to_all x1, starting transfers between devices, on_device(): all_to_all(jnp.stack([normed] * axis_size('tp')), axis_name='tp', split_a...  9.97 us
  transfers between devices with their start and end apart: 3, of which 3 were waited for; matrix products, arithmetic and copies ran while one was open for 7% of the time, Pallas kernels for 0%

profile of v1, /device:TPU:1, one launch (start us, length us, event | category | flops | bytes accessed | tf_op | source)
XLA Modules:
  0.0 328.1 jit_solution(13300442189452951738)
XLA Ops:
  7.2 0.0 copy-start
  7.2 1.4 fusion.7
  8.6 1.3 fusion.9
  9.9 2.8 stack.4
  12.7 10.0 %all-to-all-start = ((bf16[8,4,24,3072]{3,2,1,0:T(8,128)(2,1)}), bf16[8,4,24,3072]{3,2,1,0:T(8,128)(2,1)}, u32[]{:S(2)}, u32[]{:S(2)}) async-start(bf16[8,4,24,3072]{3,2,1,0:T(8,128)(2,1)} %stack.4), calls=%async_computation | async-start | bytes 9437184 | tf_op jit(solution)/shard_map/all_to_all | solution.py:37
  22.6 0.0 all-reduce.2.cloned.1.call-start
  22.6 4.3 %copy.22 = bf16[3072,384]{0,1:T(8,128)(2,1)} copy(bf16[3072,384]{1,0:T(8,128)(2,1)} %param.11) | data formatting | bytes 4718592 | tf_op args[3]
  26.9 0.0 copy-start.9
  26.9 0.0 copy-start.7
  26.9 4.3 %copy.21 = bf16[3072,384]{0,1:T(8,128)(2,1)} copy(bf16[3072,384]{1,0:T(8,128)(2,1)} %param.10) | data formatting | bytes 4718592 | tf_op args[2]
  31.2 0.1 fusion.19
  31.3 0.1 pad_maximum_fusion
  31.4 0.0 copy-done.9
  31.4 0.2 convert_reduce_fusion
  31.6 0.0 copy-done.7
  31.6 0.1 iota_compare_fusion.3
  31.6 0.2 broadcast_and_fusion
  31.8 90.7 %all-to-all-done = bf16[8,4,24,3072]{3,2,1,0:T(8,128)(2,1)} async-done(((bf16[8,4,24,3072]{3,2,1,0:T(8,128)(2,1)}), bf16[8,4,24,3072]{3,2,1,0:T(8,128)(2,1)}, u32[]{:S(2)}, u32[]{:S(2)}) %all-to-all-start) | async-done | bytes 4718624 | tf_op jit(solution)/shard_map/all_to_all | solution.py:37
  122.6 5.2 %fusion.25 = f32[32,24,4,96]{3,1,2,0:T(8,128)S(1)} fusion(bf16[32,24,3072,1]{2,1,3,0:T(8,128)(2,1)} %bitcast.4, bf16[4,96,3072,1]{2,1,0,3:T(8,128)(2,1)} %bitcast.35), kind=kOutput, calls=%fused_computation.49 | convolution fusion | flops 1811939328 | bytes 8257536 | tf_op jit(solution)/shard_map/dot_general | solution.py:49
  127.8 0.0 copy-start.2
  127.8 0.0 copy-start.5
  127.8 2.3 slice_negate_fusion
  130.1 0.1 copy-done.2
  130.2 1.0 copy-done.5
  131.2 4.5 %fusion.24 = f32[32,24,4,96]{3,1,2,0:T(8,128)S(1)} fusion(bf16[32,24,3072,1]{2,1,3,0:T(8,128)(2,1)} %bitcast.4, bf16[4,96,3072,1]{2,1,0,3:T(8,128)(2,1)S(1)} %bitcast.34), kind=kOutput, calls=%fused_computation.48 | convolution fusion | flops 1811939328 | bytes 8257536 | tf_op jit(solution)/shard_map/dot_general | solution.py:46
  135.7 0.0 copy-start.1
  135.7 0.0 copy-start.8
  135.7 2.3 slice_negate_fusion.1
  138.1 0.0 copy-done.1
  138.1 1.0 copy-done.8
  139.1 4.9 %convolution_convert_fusion.3 = bf16[768,384]{1,0:T(8,128)(2,1)S(1)} fusion(bf16[768,3072]{1,0:T(8,128)(2,1)} %bitcast, bf16[3072,384]{1,0:T(8,128)(2,1)S(1)} %copy-done.8), kind=kOutput, calls=%fused_computation.19 | convolution fusion | flops 1812234240 | bytes 7667712 | tf_op jit(solution)/shard_map/dot_general | solution.py:51
  144.0 0.0 copy-start.6
  144.0 1.5 reshape_squeeze_stack_reshape.3
  145.5 0.0 copy-done.6
  145.5 2.8 fusion.5
  148.3 1.2 copy.26
  149.6 4.9 %fusion.21 = (f32[32,4,24]{2,1,0:T(4,128)S(1)}, f32[32,4,24,24]{2,3,1,0:T(8,128)}) fusion(pred[32,24,24]{1,2,0:T(8,128)(4,1)S(1)} %broadcast_and_fusion, bf16[32,24,4,96]{3,1,2,0:T(8,128)(2,1)S(1)} %fusion.5, f32[32,24,4,48]{3,1,2,0:T(8,128)} %get-tuple-element.3, f32[32,24,4,48]{3,1,2,0:T(8,128)} %get-tuple-element.2, f32[32,24,4,96]{3,1,2,0:T(8,128)} %copy-done.1, ...), kind=kOutput, calls=%fused_computation.47 | convolution fusion | flops 15998999 | bytes 3293184 | tf_op jit(solution)/shard_map/sub | solution.py:69
  154.5 2.3 fusion.6
  156.8 0.3 copy.25
  157.1 1.3 reshape_reshape.7
  158.4 0.0 copy-done
  158.4 5.4 %convolution_convert_fusion.1 = bf16[768,3072]{1,0:T(8,128)(2,1)} fusion(bf16[768,384]{1,0:T(8,128)(2,1)} %reshape_reshape.7, bf16[384,3072]{1,0:T(8,128)(2,1)S(1)} %copy-done), kind=kOutput, calls=%fused_computation.2 | convolution fusion | flops 1814298624 | bytes 7667712 | tf_op jit(solution)/shard_map/dot_general | solution.py:91
  163.8 0.0 copy-start.4
  163.8 0.0 all-reduce.2.cloned.1.call-update
  163.9 1.1 copy-done.4
  165.0 1.3 stack_reshape.6
  166.3 1.5 maximum_select_fusion
  167.8 1.2 copy.27
  169.0 1.7 select_n.23
  170.8 3.4 %convolution_convert_fusion = bf16[64,18432]{1,0:T(8,128)(2,1)} fusion(bf16[32,18432]{1,0:T(8,128)(2,1)} %select_n.23, s32[32]{0:T(128)S(1)} %multiply_add_fusion), kind=kOutput, calls=%fused_computation.1 | convolution fusion | flops 76679168 | bytes 3539072 | tf_op jit(solution)/shard_map/dot_general | solution.py:86
  174.2 4.6 %reshape.115 = bf16[64,24,2,384]{3,2,1,0:T(2,128)(2,1)} reshape(bf16[64,18432]{1,0:T(8,128)(2,1)} %convolution_convert_fusion) | data formatting | bytes 4718592 | tf_op jit(solution)/shard_map/reshape | solution.py:89
  178.8 0.0 copy-start.3
  178.8 15.1 %all-to-all-start.1 = ((bf16[64,24,2,384]{3,2,1,0:T(2,128)(2,1)}), bf16[64,24,2,384]{3,2,1,0:T(2,128)(2,1)}, u32[]{:S(2)}, u32[]{:S(2)}) async-start(bf16[64,24,2,384]{3,2,1,0:T(2,128)(2,1)} %reshape.115), calls=%async_computation.1 | async-start | bytes 4718592 | tf_op jit(solution)/shard_map/all_to_all | solution.py:90
  193.9 58.4 %all-to-all-done.1 = bf16[64,24,2,384]{3,2,1,0:T(2,128)(2,1)} async-done(((bf16[64,24,2,384]{3,2,1,0:T(2,128)(2,1)}), bf16[64,24,2,384]{3,2,1,0:T(2,128)(2,1)}, u32[]{:S(2)}, u32[]{:S(2)}) %all-to-all-start.1) | async-done | bytes 2359328 | tf_op jit(solution)/shard_map/all_to_all | solution.py:90
  252.4 62.1 %all-reduce.2.cloned.1.call-done = bf16[32,24,3072]{2,1,0:T(8,128)(2,1)} async-done(((bf16[32,24,3072]{2,1,0:T(8,128)(2,1)}), bf16[32,24,3072]{2,1,0:T(8,128)(2,1)}) %all-reduce.2.cloned.1.call-update) | async-done | bytes 4718608 | tf_op jit(solution)/shard_map/psum | solution.py:95
  314.5 0.0 copy-done.3
  314.5 2.0 fusion.10
  316.5 4.7 %copy.34 = bf16[64,24,2,384]{3,2,1,0:T(2,128)(2,1)} copy(bf16[64,24,2,384]{3,2,1,0:T(2,128)(2,1)} %all-to-all-done.1) | data formatting | bytes 4718592
  (4 shorter events, 0.0 us)
Async XLA Ops:
  7.2 151.3 %copy-start = (bf16[384,3072]{1,0:T(8,128)(2,1)S(1)}, bf16[384,3072]{1,0:T(8,128)(2,1)}, u32[]{:S(2)}) copy-start(bf16[384,3072]{1,0:T(8,128)(2,1)} %param.13) | copy-start | bytes 7077892
  12.7 109.9 %all-to-all-start = ((bf16[8,4,24,3072]{3,2,1,0:T(8,128)(2,1)}), bf16[8,4,24,3072]{3,2,1,0:T(8,128)(2,1)}, u32[]{:S(2)}, u32[]{:S(2)}) async-start(bf16[8,4,24,3072]{3,2,1,0:T(8,128)(2,1)} %stack.4), calls=%async_computation | async-start | bytes 9437184 | tf_op jit(solution)/shard_map/all_to_all | solution.py:37
  22.6 291.9 %all-reduce.2.cloned.1.call-start = ((), (), s32[]{:S(2)}) async-start(), calls=%async_computation.2 | async-start | bytes 9437184 | tf_op jit(solution)/shard_map/psum | solution.py:95
  26.9 4.5 %copy-start.9 = (s32[1,32,1]{1,2,0:T(1,128)S(1)}, s32[1,32,1]{1,2,0:T(1,128)}, u32[]{:S(2)}) copy-start(s32[1,32,1]{1,2,0:T(1,128)} %param.15) | copy-start | bytes 388
  26.9 4.7 %copy-start.7 = (s32[1,32]{1,0:T(1,128)S(1)}, s32[1,32]{1,0:T(1,128)}, u32[]{:S(2)}) copy-start(s32[1,32]{1,0:T(1,128)} %param.14) | copy-start | bytes 388
  127.8 2.4 copy-start.2
  127.8 3.4 %copy-start.5 = (bf16[3072,384]{0,1:T(8,128)(2,1)S(1)}, bf16[3072,384]{0,1:T(8,128)(2,1)}, u32[]{:S(2)}) copy-start(bf16[3072,384]{0,1:T(8,128)(2,1)} %copy.21) | copy-start | bytes 7077892
  135.7 2.4 copy-start.1
  135.7 3.4 %copy-start.8 = (bf16[3072,384]{1,0:T(8,128)(2,1)S(1)}, bf16[3072,384]{1,0:T(8,128)(2,1)}, u32[]{:S(2)}) copy-start(bf16[3072,384]{1,0:T(8,128)(2,1)} %param.12) | copy-start | bytes 7077892
  144.0 1.5 copy-start.6
  163.8 1.1 copy-start.4
  178.8 135.7 %copy-start.3 = (bf16[4,24,3072]{2,1,0:T(8,128)(2,1)S(1)}, bf16[4,24,3072]{2,1,0:T(8,128)(2,1)}, u32[]{:S(2)}) copy-start(bf16[4,24,3072]{2,1,0:T(8,128)(2,1)} %param.8) | copy-start | bytes 1769476
  178.8 73.5 %all-to-all-start.1 = ((bf16[64,24,2,384]{3,2,1,0:T(2,128)(2,1)}), bf16[64,24,2,384]{3,2,1,0:T(2,128)(2,1)}, u32[]{:S(2)}, u32[]{:S(2)}) async-start(bf16[64,24,2,384]{3,2,1,0:T(2,128)(2,1)} %reshape.115), calls=%async_computation.1 | async-start | bytes 4718592 | tf_op jit(solution)/shard_map/all_to_all | solution.py:90
Sparse Core Ops, SparseCore 0:
  164.0 150.4 all-reduce.1
